TPU v7x, 512 devices: a whole 4x4x16 slice. The times are simulated.
512 devices in a mesh: rep: 8 (over z_lo), fsdp: 64 (over z_hi, x, y, core).
Axes of the slice: x: 4, y: 4, z: 16 (z_hi: 2, z_lo: 8; z = z_hi * 8 + z_lo), core: 2. Of those that a mesh axis runs over, the one named last changes fastest.
Arguments:
- base_weights: bfloat16 [4096, 8192], P('fsdp'), may hold values from -6 to 6
- local_weights: bfloat16 [8, 4096, 8192], P('rep', 'fsdp'), may hold values from -6 to 6
- outer_params: float32 [4096, 8192], P('rep', 'fsdp'), may hold values from -6 to 6
- momentum: float32 [4096, 8192], P('rep', 'fsdp'), may hold values from -4 to 4
Outputs:
- new_outer: float32 [4096, 8192], P('rep', 'fsdp')
- new_momentum: float32 [4096, 8192], P('rep', 'fsdp')
- new_weights: bfloat16 [4096, 8192], P('fsdp')
All inputs are finite; a program needn't handle non-finite values.
Results may differ from a plain program's by a relative error of at most 0.012.
Values may be sent and summed in bfloat16 or wider, within the bound.
A program may use at most 64 MiB of HBM per device.

v0:
```python
import jax
import jax.numpy as jnp
from jax import lax
from jax.sharding import Mesh
from jax.sharding import PartitionSpec as P

BLOCK = 128
FSDP = ("fsdp_0", "fsdp_1", "fsdp_2", "fsdp_3")


LEVEL_LIMIT = 448.0
EPSILON = 1e-06
OUTER_RATE = 0.7
MOMENTUM_DECAY = 0.9


def in_one_piece(arrays, axis, split_dim, concat_dim, along):
    ends, at = ([], 0)
    for a in arrays[:-1]:
        at += a.shape[along]
        ends.append(at)
    both = jnp.concatenate(arrays, axis=along)
    return tuple(
        jnp.split(
            lax.all_to_all(both, axis, split_axis=split_dim, concat_axis=concat_dim, tiled=True),
            ends,
            axis=along,
        )
    )


def cut_along(x, dim, peers):
    before, after = (x.shape[:dim], x.shape[dim + 1 :])
    return jnp.moveaxis(x.reshape(*before, peers, -1, *after), dim, 0)


def laid_out(pieces, dim):
    pieces = jnp.moveaxis(pieces, 0, dim)
    shape = pieces.shape
    return pieces.reshape(*shape[:dim], shape[dim] * shape[dim + 1], *shape[dim + 2 :])


def exchange_in_order(pieces, axes, turns):
    inside = pieces.shape[1:]
    out = pieces.reshape(*(lax.axis_size(a) for a in axes), *inside)
    for k in turns:
        out = lax.all_to_all(out, axes[k], k, k, tiled=True)
    return out.reshape(-1, *inside)


def exchange_by_chip(x, groups, turns, split_dim, concat_dim):
    peers = lax.axis_size(groups[0]) * lax.axis_size(groups[1])
    pieces = cut_along(x, split_dim, peers)
    return laid_out(exchange_in_order(pieces, groups, turns), concat_dim)


def from_everyone(x, axis):
    peers = lax.axis_size(axis)
    return lax.all_to_all(jnp.broadcast_to(x[None], (peers, *x.shape)), axis, 0, 0, tiled=True)


def gather_directly(x, axis, dim):
    pieces = from_everyone(x, axis)
    return laid_out(pieces, dim)


def per_device(base_weights, local_weights, outer_params, momentum):
    local_shard = local_weights[0]
    row_count, full_width = local_shard.shape
    pseudo = base_weights.astype(jnp.float32) - local_shard.astype(jnp.float32)
    blocks = pseudo.reshape(row_count, full_width // BLOCK, BLOCK)
    largest = jnp.max(jnp.abs(blocks), axis=2)
    scales = ((largest + EPSILON) / LEVEL_LIMIT).astype(jnp.bfloat16)
    levels = (blocks / scales.astype(jnp.float32)[:, :, None]).astype(jnp.bfloat16)
    levels = levels.reshape(row_count, full_width)
    replica_count = lax.axis_size("rep")
    fsdp_count = lax.axis_size(FSDP)
    got_levels, got_scales = in_one_piece((levels[None], scales[None]), "rep", 1, 0, 2)
    share = row_count // replica_count
    block_count = got_scales.shape[2]
    wide = got_levels.astype(jnp.float32).reshape(replica_count, share, block_count, BLOCK)
    weighted = wide * got_scales.astype(jnp.float32)[:, :, :, None]
    row_sums = jnp.sum(weighted, axis=0).reshape(share, full_width)
    by_column = exchange_by_chip(
        row_sums[None].astype(jnp.bfloat16),
        (("fsdp_0", "fsdp_1", "fsdp_2"), "fsdp_3"),
        (1, 0),
        2,
        0,
    ).astype(jnp.float32)
    column_width = by_column.shape[2]
    group = fsdp_count // replica_count
    grouped = by_column.reshape(replica_count, group, share, column_width)[None]
    owned_parts = lax.all_to_all(
        grouped.astype(jnp.bfloat16), "rep", split_axis=1, concat_axis=0, tiled=True
    ).astype(grouped.dtype)
    owned_parts = owned_parts.reshape(replica_count, group, share, column_width)
    summed = jnp.transpose(owned_parts, (1, 0, 2, 3)).reshape(
        group * replica_count * share, column_width
    )
    average = summed / replica_count
    new_momentum = MOMENTUM_DECAY * momentum + average
    new_outer = outer_params - OUTER_RATE * (average + MOMENTUM_DECAY * new_momentum)
    narrow = new_outer.astype(jnp.bfloat16)
    column_block = gather_directly(narrow, "rep", 0)
    new_weights = lax.all_to_all(column_block, FSDP, split_axis=0, concat_axis=1, tiled=True)
    return (new_outer, new_momentum, new_weights)


def solution(mesh):
    finer = Mesh(
        mesh.devices.reshape(mesh.shape["rep"], 2, 4, 4, 2),
        ("rep", "fsdp_0", "fsdp_1", "fsdp_2", "fsdp_3"),
    )
    placed = (P(FSDP, None), P("rep", FSDP, None), P("rep", FSDP), P("rep", FSDP))
    return jax.shard_map(
        per_device,
        mesh=finer,
        in_specs=placed,
        out_specs=(P("rep", FSDP), P("rep", FSDP), P(FSDP, None)),
        check_vma=False,
    )
```

profile of v0, /device:TPU:35, one launch (start us, length us, event | category | flops | bytes accessed | tf_op | source)
XLA Modules:
  0.0 253.6 jit_solution(5506472094887441765)
XLA Ops:
  0.6 1.8 abs_bitcast_fusion
  2.5 0.4 copy.26
  2.8 0.0 copy-start
  2.9 0.6 reduce_max.9
  3.5 0.0 copy-start.1
  3.5 0.6 div.32
  4.1 0.0 copy-done
  4.1 0.7 copy-done.1
  4.8 1.5 fusion.2
  6.3 0.1 pad_maximum_fusion
  6.4 1.6 copy.36
  8.1 0.5 broadcast.47
  8.6 7.5 %reduce.1 = bf16[64,8256]{1,0:T(8,128)(2,1)S(1)} reduce(bf16[64,1,8256]{2,1,0:T(2,128)(2,1)S(1)} %bitcast.59, bf16[]{:T(256)} %broadcast.47), dimensions={1}, to_apply=%bitcast.58.reduce_sub_computation | reduce | bytes 2113538
  16.1 0.9 reshape.93
  17.1 61.1 %all_to_all.55 = bf16[8,2,33024]{2,1,0:T(2,128)(2,1)S(1)} all-to-all(bf16[8,2,33024]{2,1,0:T(2,128)(2,1)S(1)} %reshape.93), channel_id=1, replica_groups=mesh['rep'=8,'fsdp_0'=2,'fsdp_1'=4,'fsdp_2'=4,'fsdp_3'=2] {'rep'}, dimensions={0} | all-to-all | bytes 2113536 | tf_op jit(solution)/shard_map/all_to_all | solution.py:25
  78.2 2.3 reshape.94
  80.5 0.1 copy.35
  80.6 0.0 copy-start.2
  80.7 0.0 copy-start.3
  80.7 0.1 copy.18
  80.8 0.7 fusion.1
  81.6 5.5 %all_to_all.56 = bf16[32,2,1,8,128]{4,3,0,2,1:T(8,128)(2,1)S(1)} all-to-all(bf16[32,2,1,8,128]{4,3,0,2,1:T(8,128)(2,1)S(1)} %copy.19), channel_id=1, replica_groups=mesh['rep'=8,'fsdp_0'=2,'fsdp_1'=4,'fsdp_2'=4,'fsdp_3'=2] {'fsdp_3'}, dimensions={1} | all-to-all | bytes 262144 | tf_op jit(solution)/shard_map/all_to_all | solution.py:47
  87.1 32.4 %all_to_all.57 = bf16[32,2,1,8,128]{4,3,1,2,0:T(8,128)(2,1)S(1)} all-to-all(bf16[32,2,1,8,128]{4,3,1,2,0:T(8,128)(2,1)S(1)} %copy.20), channel_id=1, replica_groups=mesh['rep'=8,'fsdp_0'=2,'fsdp_1'=4,'fsdp_2'=4,'fsdp_3'=2] {'fsdp_0','fsd..., dimensions={0} | all-to-all | bytes 262144 | tf_op jit(solution)/shard_map/all_to_all | solution.py:47
  119.5 11.3 %all_to_all.58 = bf16[1,8,8,8,128]{4,3,2,0,1:T(8,128)(2,1)S(1)} all-to-all(bf16[1,8,8,8,128]{4,3,2,0,1:T(8,128)(2,1)S(1)} %bitcast.66), channel_id=1, replica_groups=mesh['rep'=8,'fsdp_0'=2,'fsdp_1'=4,'fsdp_2'=4,'fsdp_3'=2] {'rep'}, dimensions={1} | all-to-all | bytes 262144 | tf_op jit(solution)/shard_map/all_to_all | solution.py:94
  130.8 0.0 copy-done.2
  130.8 0.0 copy-done.3
  130.9 0.9 fusion.7
  131.7 0.1 broadcast_in_dim.2
  131.9 54.1 %all_to_all.59 = bf16[8,512,128]{2,1,0:T(8,128)(2,1)S(1)} all-to-all(bf16[8,512,128]{2,1,0:T(8,128)(2,1)S(1)} %broadcast_in_dim.2), channel_id=1, replica_groups=mesh['rep'=8,'fsdp_0'=2,'fsdp_1'=4,'fsdp_2'=4,'fsdp_3'=2] {'rep'}, dimensions={0} | all-to-all | bytes 2097152 | tf_op jit(solution)/shard_map/all_to_all | solution.py:59
  185.9 66.6 %all_to_all.60 = bf16[64,64,128]{2,1,0:T(8,128)(2,1)S(1)} all-to-all(bf16[64,64,128]{2,1,0:T(8,128)(2,1)S(1)} %bitcast.65), channel_id=1, replica_groups=mesh['rep'=8,'fsdp_0'=2,'fsdp_1'=4,'fsdp_2'=4,'fsdp_3'=2] {'fsdp_0','fsd..., dimensions={0} | all-to-all | bytes 2097152 | tf_op jit(solution)/shard_map/all_to_all | solution.py:106
  252.5 1.1 copy_bitcast_fusion.1
  (5 shorter events, 0.1 us)
Async XLA Ops:
  2.8 1.3 copy-start
  3.5 1.3 copy-start.1
  80.6 50.2 %copy-start.2 = (f32[512,128]{1,0:T(8,128)S(1)}, f32[512,128]{1,0:T(8,128)}, u32[]{:S(2)}) copy-start(f32[512,128]{1,0:T(8,128)} %param.6) | copy-start | bytes 786436
  80.7 50.2 %copy-start.3 = (f32[512,128]{1,0:T(8,128)S(1)}, f32[512,128]{1,0:T(8,128)}, u32[]{:S(2)}) copy-start(f32[512,128]{1,0:T(8,128)} %param.7) | copy-start | bytes 786436
where the time goes:
time: 254 us
  blocking collectives  231 us (91%)
  other arithmetic  13.2 us (5%)
  local copies, waits for them, and re-layouts  8.59 us (3%)
    all_to_all x1, blocking collectives, per_device(): lax.all_to_all(column_block, FSDP, split_axis=0, concat_axis=1, tiled=True)  66.6 us
    all_to_all x1, blocking collectives, in_one_piece(): lax.all_to_all(both, axis, split_axis=split_dim, concat_axis=concat_dim,...  61.1 us
    all_to_all x1, blocking collectives, from_everyone(): lax.all_to_all(jnp.broadcast_to(x[None], (peers, *x.shape)), axis, 0, 0,...  54.1 us
    all_to_all x2, blocking collectives, exchange_in_order(): out = lax.all_to_all(out, axes[k], k, k, tiled=True)  37.9 us
    all_to_all x1, blocking collectives, per_device(): lax.all_to_all(grouped.astype(jnp.bfloat16), 'rep', split_axis=1, concat_...  11.3 us
    unnamed x2, other arithmetic  9.36 us

commit v1 on v0

v1 whole, which is shorter than its diff:
```python
import functools

import jax
import jax.numpy as jnp
from jax import lax
from jax.experimental import pallas as pl
from jax.experimental.pallas import tpu as pltpu
from jax.sharding import Mesh
from jax.sharding import PartitionSpec as P

BLOCK = 128
LEVEL_LIMIT = 448.0
EPSILON = 1e-06
OUTER_RATE = 0.7
MOMENTUM_DECAY = 0.9
MESH = pl.DeviceIdType.MESH

FROM_MOMENTUM = OUTER_RATE * MOMENTUM_DECAY * MOMENTUM_DECAY
FROM_AVERAGE = OUTER_RATE * (1.0 + MOMENTUM_DECAY)

PARTS = 4
LAG = 4
GATHER_PARTS = 4


def kernel(n, base_hbm, local_hbm, outer_hbm, momentum_hbm, new_outer_hbm, new_momentum_hbm, weights_hbm,
           base, local, outer, momentum, new_outer, new_momentum,
           own, sums, from_left, from_right, gathered, prior_out, prior_in, total_out, total_in,
           in_sem, out_sem, right_send, right_recv, left_send, left_recv,
           prior_send, prior_recv, total_send, total_recv, ag_right_send, ag_left_send, ag_recv, weights_sem):
    a, b, l = lax.axis_index("rep"), lax.axis_index("hi"), lax.axis_index("lo")
    last = n - 1
    per_chunk = own.shape[0]
    wide = per_chunk // PARTS
    mirrored = a == b

    ins = [
        pltpu.make_async_copy(src, dst, in_sem.at[k])
        for k, (src, dst) in enumerate(
            ((outer_hbm, outer), (momentum_hbm, momentum), (base_hbm, base), (local_hbm, local))
        )
    ]
    for copy in ins:
        copy.start()

    barrier = pltpu.get_barrier_semaphore()

    @pl.when(a > 0)
    def _():
        pl.semaphore_signal(barrier, inc=1, device_id={"rep": a - 1}, device_id_type=MESH)

    @pl.when(a < last)
    def _():
        pl.semaphore_signal(barrier, inc=1, device_id={"rep": a + 1}, device_id_type=MESH)

    for j in range(n):
        @pl.when(jnp.logical_not(mirrored & (l == j)))
        def _():
            pl.semaphore_signal(barrier, inc=1, device_id=(b, a, j), device_id_type=MESH)

    greeted = n + 2 - (a == 0).astype(jnp.int32) - (a == last).astype(jnp.int32) - mirrored.astype(jnp.int32)

    def exchange(j, src, dst, send_sem, recv_sem):
        return pltpu.make_async_remote_copy(
            src_ref=src.at[j], dst_ref=dst.at[l], send_sem=send_sem.at[j], recv_sem=recv_sem.at[l],
            device_id=(b, a, j), device_id_type=MESH)

    def keep(j, src, dst, recv_sem):
        return pltpu.make_async_copy(src.at[j], dst.at[j], recv_sem.at[j])

    def start_exchange(j, src, dst, send_sem, recv_sem):
        mine = mirrored & (l == j)

        @pl.when(mine)
        def _():
            keep(j, src, dst, recv_sem).start()

        @pl.when(jnp.logical_not(mine))
        def _():
            exchange(j, src, dst, send_sem, recv_sem).start()

    def wait_exchange(j, src, dst, send_sem, recv_sem):
        mine = mirrored & (l == j)

        @pl.when(mine)
        def _():
            keep(j, src, dst, recv_sem).wait()

        @pl.when(jnp.logical_not(mine))
        def _():
            pltpu.make_async_remote_copy(
                src_ref=src.at[j], dst_ref=dst.at[j], send_sem=send_sem.at[j], recv_sem=recv_sem.at[j],
                device_id=(b, a, j), device_id_type=MESH).wait_recv()

    def wait_sent(j, src, dst, send_sem, recv_sem):
        @pl.when(jnp.logical_not(mirrored & (l == j)))
        def _():
            exchange(j, src, dst, send_sem, recv_sem).wait_send()

    def dequantized(block):
        columns = pl.ds(pl.multiple_of(block * BLOCK, BLOCK), BLOCK)
        pseudo = base[:, columns].astype(jnp.float32) - local[:, columns].astype(jnp.float32)
        largest = jnp.max(jnp.abs(pseudo), axis=1, keepdims=True)
        scale = ((largest + EPSILON) / LEVEL_LIMIT).astype(jnp.bfloat16).astype(jnp.float32)
        levels = (pseudo / scale).astype(jnp.bfloat16).astype(jnp.float32)
        return levels * scale

    ins[0].wait()
    ins[1].wait()
    rows = prior_out.shape[1]
    for j in range(n):
        part = pl.ds(j * rows, rows)
        prior_out[j] = (outer[part, :] - FROM_MOMENTUM * momentum[part, :]).astype(jnp.bfloat16)
    pl.semaphore_wait(barrier, greeted)
    prior = (prior_out, prior_in, prior_send, prior_recv)
    for j in range(n):
        start_exchange(j, *prior)
    ins[2].wait()
    ins[3].wait()

    def passed_on(arrived, send_sem, recv_sem, block, to):
        return pltpu.make_async_remote_copy(
            src_ref=sums.at[pl.ds(block, wide)], dst_ref=arrived.at[pl.ds(block, wide)],
            send_sem=send_sem.at[block // wide], recv_sem=recv_sem.at[block // wide],
            device_id={"rep": to}, device_id_type=MESH)

    def pass_on(has_input, arrived, send_sem, recv_sem, block, to):
        copy = passed_on(arrived, send_sem, recv_sem, block, to)
        for k in range(wide):
            own[k] = dequantized(block + k)

        @pl.when(has_input)
        def _():
            copy.wait_recv()
            for k in range(wide):
                sums[block + k] = (own[k] + arrived[block + k].astype(jnp.float32)).astype(jnp.bfloat16)

        @pl.when(jnp.logical_not(has_input))
        def _():
            for k in range(wide):
                sums[block + k] = own[k].astype(jnp.bfloat16)

        copy.start()

    def right_block(u):
        return ((last - u // PARTS) * PARTS + u % PARTS) * wide

    def left_block(v):
        return v * wide

    right_to, left_to = jnp.minimum(a + 1, last), jnp.maximum(a - 1, 0)
    right = (from_left, right_send, right_recv)
    left = (from_right, left_send, left_recv)
    right_count, left_count = (last - a) * PARTS, a * PARTS

    def step(t, carry):
        u, v = t - a * LAG, t - (last - a) * LAG

        @pl.when((u >= 0) & (u < right_count))
        def _():
            pass_on(a > 0, *right, right_block(u), right_to)

        @pl.when((v >= 0) & (v < left_count))
        def _():
            pass_on(a < last, *left, left_block(v), left_to)

        return carry

    lax.fori_loop(0, last * max(LAG, PARTS), step, None)

    for j in range(n):
        own[j] = dequantized(a * per_chunk + j)
    for j in range(n):
        wait_exchange(j, *prior)
    totals = (total_out, total_in, total_send, total_recv)
    gather_wide = per_chunk // GATHER_PARTS

    def gather_copy(block, send_sem, to):
        return pltpu.make_async_remote_copy(
            src_ref=gathered.at[pl.ds(block, gather_wide)], dst_ref=gathered.at[pl.ds(block, gather_wide)],
            send_sem=send_sem.at[block // gather_wide], recv_sem=ag_recv.at[block // gather_wide],
            device_id={"rep": to}, device_id_type=MESH)

    def write_out(block):
        columns = pl.ds(pl.multiple_of(block * BLOCK, BLOCK), BLOCK)
        return pltpu.make_async_copy(gathered.at[block], weights_hbm.at[:, columns], weights_sem.at[block])

    def hand_on(block):
        @pl.when(a < last)
        def _():
            gather_copy(block, ag_right_send, right_to).start()

        @pl.when(a > 0)
        def _():
            gather_copy(block, ag_left_send, left_to).start()

    for q in range(PARTS):
        block = a * per_chunk + q * wide

        @pl.when(a > 0)
        def _():
            passed_on(from_left, right_send, right_recv, block, right_to).wait_recv()
            for k in range(wide):
                own[q * wide + k] += from_left[block + k].astype(jnp.float32)

        @pl.when(a < last)
        def _():
            passed_on(from_right, left_send, left_recv, block, left_to).wait_recv()
            for k in range(wide):
                own[q * wide + k] += from_right[block + k].astype(jnp.float32)

        for k in range(wide):
            j = q * wide + k
            total = own[j]
            total_out[j] = total.astype(jnp.bfloat16)
            gathered[block + k] = (
                prior_in[j].astype(jnp.float32) - (FROM_AVERAGE / n) * total).astype(jnp.bfloat16)
        hand_on(block)
        for k in range(wide):
            start_exchange(q * wide + k, *totals)
    for j in range(n):
        write_out(a * per_chunk + j).start()

    for s in range(1, n):
        for q in range(GATHER_PARTS):
            @pl.when(a - s >= 0)
            def _():
                block = (a - s) * per_chunk + q * gather_wide
                gather_copy(block, ag_right_send, right_to).wait_recv()

                @pl.when(a < last)
                def _():
                    gather_copy(block, ag_right_send, right_to).start()

                for k in range(gather_wide):
                    write_out(block + k).start()

            @pl.when(a + s <= last)
            def _():
                block = (a + s) * per_chunk + q * gather_wide
                gather_copy(block, ag_left_send, left_to).wait_recv()

                @pl.when(a > 0)
                def _():
                    gather_copy(block, ag_left_send, left_to).start()

                for k in range(gather_wide):
                    write_out(block + k).start()

        if s == n - 3:
            for j in range(n):
                wait_exchange(j, *totals)
                part = pl.ds(j * rows, rows)
                average = total_in[j].astype(jnp.float32) / n
                moved = MOMENTUM_DECAY * momentum[part, :] + average
                new_momentum[part, :] = moved
                new_outer[part, :] = outer[part, :] - OUTER_RATE * (average + MOMENTUM_DECAY * moved)
            pltpu.make_async_copy(new_outer, new_outer_hbm, out_sem.at[0]).start()
            pltpu.make_async_copy(new_momentum, new_momentum_hbm, out_sem.at[1]).start()

    pltpu.make_async_copy(new_outer, new_outer_hbm, out_sem.at[0]).wait()
    pltpu.make_async_copy(new_momentum, new_momentum_hbm, out_sem.at[1]).wait()
    for j in range(n):
        wait_sent(j, *prior)
        wait_sent(j, *totals)

    def drain(block, carry):
        write_out(block).wait()
        return carry

    lax.fori_loop(0, n * per_chunk, drain, None)

    def drain_sums(piece, carry):
        block = piece * wide
        chunk = piece // PARTS

        @pl.when(chunk > a)
        def _():
            passed_on(from_left, right_send, right_recv, block, right_to).wait_send()

        @pl.when(chunk < a)
        def _():
            passed_on(from_right, left_send, left_recv, block, left_to).wait_send()

        return carry

    lax.fori_loop(0, n * PARTS, drain_sums, None)

    def drain_gather(piece, carry):
        block = piece * gather_wide
        chunk = piece // GATHER_PARTS

        @pl.when((chunk <= a) & (a < last))
        def _():
            gather_copy(block, ag_right_send, right_to).wait_send()

        @pl.when((chunk >= a) & (a > 0))
        def _():
            gather_copy(block, ag_left_send, left_to).wait_send()

        return carry

    lax.fori_loop(0, n * GATHER_PARTS, drain_gather, None)


def solution(mesh):
    n = mesh.shape["rep"]
    finer = Mesh(mesh.devices.reshape(n, n, -1), ("rep", "hi", "lo"))

    def per_device(base_weights, local_weights, outer_params, momentum):
        rows, width = base_weights.shape
        blocks = width // BLOCK
        per_chunk = blocks // n
        bf16, f32 = jnp.bfloat16, jnp.float32
        held = pltpu.VMEM((blocks, rows, BLOCK), bf16)
        eight = pltpu.VMEM((n, rows, BLOCK), bf16)
        owned = outer_params.shape
        dma = pltpu.SemaphoreType.DMA
        anywhere = pl.BlockSpec(memory_space=pl.ANY)
        pieces, gather_pieces = n * PARTS, n * GATHER_PARTS
        return pl.pallas_call(
            functools.partial(kernel, n),
            out_shape=(
                jax.ShapeDtypeStruct(owned, f32),
                jax.ShapeDtypeStruct(owned, f32),
                jax.ShapeDtypeStruct((rows, width), bf16),
            ),
            in_specs=[anywhere] * 4,
            out_specs=(anywhere,) * 3,
            scratch_shapes=[
                pltpu.VMEM((rows, width), bf16), pltpu.VMEM((rows, width), bf16),
                pltpu.VMEM(owned, f32), pltpu.VMEM(owned, f32), pltpu.VMEM(owned, f32), pltpu.VMEM(owned, f32),
                pltpu.VMEM((per_chunk, rows, BLOCK), f32), held, held, held, held,
                eight, eight, eight, eight,
                dma((4,)), dma((2,)), dma((pieces,)), dma((pieces,)), dma((pieces,)), dma((pieces,)),
                dma((n,)), dma((n,)), dma((n,)), dma((n,)),
                dma((gather_pieces,)), dma((gather_pieces,)), dma((gather_pieces,)), dma((blocks,)),
            ],
            compiler_params=pltpu.CompilerParams(collective_id=0, has_side_effects=True),
        )(base_weights, local_weights[0], outer_params, momentum)

    fsdp = ("hi", "lo")
    return jax.shard_map(
        per_device,
        mesh=finer,
        in_specs=(P(fsdp, None), P("rep", fsdp, None), P("rep", fsdp), P("rep", fsdp)),
        out_specs=(P("rep", fsdp), P("rep", fsdp), P(fsdp, None)),
        check_vma=False,
    )
```

time: 254 us -> 90.9 us (0.36)
  the two profiles are of different devices: /device:TPU:35 before, /device:TPU:16 now
where the time goes in v1:
time: 90.9 us; the launch traced here: 90.7 us
  Pallas kernels  85.7 us (94%)
  local copies, waits for them, and re-layouts  4.4 us (5%)
    pallas_call x1, Pallas kernels, per_device(): pl.pallas_call(functools.partial(kernel, n), out_shape=(jax.ShapeDtypeStr...  85.7 us
    unnamed x5, local copies, waits for them, and re-layouts  4.4 us

profile of v1, /device:TPU:16, one launch (start us, length us, event | category | flops | bytes accessed | tf_op | source)
XLA Modules:
  0.0 90.7 jit_solution(13124877264090133406)
XLA Ops:
  0.6 85.7 %shard_map.67 = (f32[512,128]{1,0:T(8,128)}, f32[512,128]{1,0:T(8,128)}, bf16[64,8192]{1,0:T(8,128)(2,1)}) custom-call(bf16[64,8192]{1,0:T(8,128)(2,1)} %base_hbm.1, bf16[64,8192]{1,0:T(8,128)(2,1)} %bitcast.1, f32[512,128]{1,0:T(8,128)} %outer_hbm.1, f32[512,128]{1,0:T(8,128)} %momentum_hbm.1), custom_call_target="tpu_custom_call" | custom-call | tf_op jit(solution)/shard_map/pallas_call | solution.py:321
  86.3 0.0 copy-start
  86.3 1.8 %copy.10 = f32[512,128]{1,0:T(8,128)} copy(f32[512,128]{1,0:T(8,128)} %get-tuple-element.6) | data formatting | bytes 524288
  88.1 1.7 %copy.11 = f32[512,128]{1,0:T(8,128)} copy(f32[512,128]{1,0:T(8,128)} %get-tuple-element.7) | data formatting | bytes 524288
  89.7 0.0 copy-done
  89.7 1.0 %copy.12 = bf16[64,8192]{1,0:T(8,128)(2,1)} copy(bf16[64,8192]{1,0:T(8,128)(2,1)S(1)} %copy-done) | data formatting | bytes 2097152
Async XLA Ops:
  86.3 3.4 %copy-start = (bf16[64,8192]{1,0:T(8,128)(2,1)S(1)}, bf16[64,8192]{1,0:T(8,128)(2,1)}, u32[]{:S(2)}) copy-start(bf16[64,8192]{1,0:T(8,128)(2,1)} %get-tuple-element.8) | copy-start | bytes 3145732

commit v2 on v1

v2 whole, which is shorter than its diff:
```python
import functools

import jax
import jax.numpy as jnp
from jax import lax
from jax.experimental import pallas as pl
from jax.experimental.pallas import tpu as pltpu
from jax.sharding import Mesh
from jax.sharding import PartitionSpec as P

BLOCK = 128
LEVEL_LIMIT = 448.0
EPSILON = 1e-06
OUTER_RATE = 0.7
MOMENTUM_DECAY = 0.9
MESH = pl.DeviceIdType.MESH

FROM_MOMENTUM = OUTER_RATE * MOMENTUM_DECAY * MOMENTUM_DECAY
FROM_AVERAGE = OUTER_RATE * (1.0 + MOMENTUM_DECAY)

PARTS = 4
LAG = 4
GATHER_PARTS = 4


def kernel(n, base_hbm, local_hbm, outer_hbm, momentum_hbm, totals_hbm, weights_hbm,
           base, local, outer, momentum,
           own, sums, from_left, from_right, gathered, prior_out, prior_in, total_out, total_in,
           in_sem, out_sem, right_send, right_recv, left_send, left_recv,
           prior_send, prior_recv, total_send, total_recv, ag_right_send, ag_left_send, ag_recv, weights_sem):
    a, b, l = lax.axis_index("rep"), lax.axis_index("hi"), lax.axis_index("lo")
    last = n - 1
    per_chunk = own.shape[0]
    wide = per_chunk // PARTS
    half = n // 2

    line_half = b // half

    def chunk_of(rank):
        near = line_half * half + rank - 2
        at_start = (1 - line_half) * half + b % 2 + 2 * rank
        at_end = (1 - line_half) * half + 1 - b % 2 + 2 * (rank - (n - 2))
        return jnp.where(rank < 2, at_start, jnp.where(rank >= n - 2, at_end, near))

    mine = chunk_of(a)
    is_near = a // half == b // half
    from_end = b % half // 2
    root = jnp.where(is_near, b % half + 2, jnp.where((a + b) % 2 == 0, from_end, n - 2 + from_end))

    ins = [
        pltpu.make_async_copy(src, dst, in_sem.at[k])
        for k, (src, dst) in enumerate(
            ((outer_hbm, outer), (momentum_hbm, momentum), (base_hbm, base), (local_hbm, local))
        )
    ]
    for copy in ins:
        copy.start()

    barrier = pltpu.get_barrier_semaphore()

    @pl.when(a > 0)
    def _():
        pl.semaphore_signal(barrier, inc=1, device_id={"rep": a - 1}, device_id_type=MESH)

    @pl.when(a < last)
    def _():
        pl.semaphore_signal(barrier, inc=1, device_id={"rep": a + 1}, device_id_type=MESH)

    for j in range(n):
        pl.semaphore_signal(barrier, inc=1, device_id=(root, a, j), device_id_type=MESH)
        pl.semaphore_signal(barrier, inc=1, device_id=(b, mine, j), device_id_type=MESH)

    greeted = 2 * n + 2 - (a == 0).astype(jnp.int32) - (a == last).astype(jnp.int32)

    def prior_copy(j):
        return pltpu.make_async_remote_copy(
            src_ref=prior_out.at[j], dst_ref=prior_in.at[l], send_sem=prior_send.at[j],
            recv_sem=prior_recv.at[l], device_id=(root, a, j), device_id_type=MESH)

    def prior_arrival(j):
        return pltpu.make_async_remote_copy(
            src_ref=prior_out.at[j], dst_ref=prior_in.at[j], send_sem=prior_send.at[j],
            recv_sem=prior_recv.at[j], device_id=(root, a, j), device_id_type=MESH)

    def total_copy(j):
        return pltpu.make_async_remote_copy(
            src_ref=total_out.at[j], dst_ref=total_in.at[l], send_sem=total_send.at[j],
            recv_sem=total_recv.at[l], device_id=(b, mine, j), device_id_type=MESH)

    def total_arrival(j):
        return pltpu.make_async_remote_copy(
            src_ref=total_out.at[j], dst_ref=total_in.at[j], send_sem=total_send.at[j],
            recv_sem=total_recv.at[j], device_id=(b, mine, j), device_id_type=MESH)

    def columns_of(block):
        return pl.ds(pl.multiple_of((chunk_of(block // per_chunk) * per_chunk + block % per_chunk) * BLOCK, BLOCK), BLOCK)

    def dequantized(block):
        columns = columns_of(block)
        pseudo = base[:, columns].astype(jnp.float32) - local[:, columns].astype(jnp.float32)
        largest = jnp.max(jnp.abs(pseudo), axis=1, keepdims=True)
        scale = ((largest + EPSILON) / LEVEL_LIMIT).astype(jnp.bfloat16).astype(jnp.float32)
        levels = (pseudo / scale).astype(jnp.bfloat16).astype(jnp.float32)
        return levels * scale

    ins[0].wait()
    ins[1].wait()
    rows = prior_out.shape[1]
    for j in range(n):
        part = pl.ds(j * rows, rows)
        prior_out[j] = (outer[part, :] - FROM_MOMENTUM * momentum[part, :]).astype(jnp.bfloat16)
    pl.semaphore_wait(barrier, greeted)
    for j in range(n):
        prior_copy(j).start()
    ins[2].wait()
    ins[3].wait()

    def passed_on(arrived, send_sem, recv_sem, block, to):
        return pltpu.make_async_remote_copy(
            src_ref=sums.at[pl.ds(block, wide)], dst_ref=arrived.at[pl.ds(block, wide)],
            send_sem=send_sem.at[block // wide], recv_sem=recv_sem.at[block // wide],
            device_id={"rep": to}, device_id_type=MESH)

    def pass_on(has_input, arrived, send_sem, recv_sem, block, to):
        copy = passed_on(arrived, send_sem, recv_sem, block, to)
        for k in range(wide):
            own[k] = dequantized(block + k)

        @pl.when(has_input)
        def _():
            copy.wait_recv()
            for k in range(wide):
                sums[block + k] = (own[k] + arrived[block + k].astype(jnp.float32)).astype(jnp.bfloat16)

        @pl.when(jnp.logical_not(has_input))
        def _():
            for k in range(wide):
                sums[block + k] = own[k].astype(jnp.bfloat16)

        copy.start()

    def right_block(u):
        return ((last - u // PARTS) * PARTS + u % PARTS) * wide

    def left_block(v):
        return v * wide

    right_to, left_to = jnp.minimum(a + 1, last), jnp.maximum(a - 1, 0)
    right = (from_left, right_send, right_recv)
    left = (from_right, left_send, left_recv)
    right_count, left_count = (last - a) * PARTS, a * PARTS

    def step(t, carry):
        u, v = t - a * LAG, t - (last - a) * LAG

        @pl.when((u >= 0) & (u < right_count))
        def _():
            pass_on(a > 0, *right, right_block(u), right_to)

        @pl.when((v >= 0) & (v < left_count))
        def _():
            pass_on(a < last, *left, left_block(v), left_to)

        return carry

    lax.fori_loop(0, n * max(LAG, PARTS), step, None)

    gather_wide = per_chunk // GATHER_PARTS

    def gather_copy(block, send_sem, to):
        return pltpu.make_async_remote_copy(
            src_ref=gathered.at[pl.ds(block, gather_wide)], dst_ref=gathered.at[pl.ds(block, gather_wide)],
            send_sem=send_sem.at[block // gather_wide], recv_sem=ag_recv.at[block // gather_wide],
            device_id={"rep": to}, device_id_type=MESH)

    def write_out(block):
        return pltpu.make_async_copy(gathered.at[block], weights_hbm.at[:, columns_of(block)], weights_sem.at[block])

    for j in range(n):
        own[j] = dequantized(a * per_chunk + j)
    for q in range(PARTS):
        block = a * per_chunk + q * wide

        @pl.when(a > 0)
        def _():
            passed_on(from_left, right_send, right_recv, block, right_to).wait_recv()
            for k in range(wide):
                own[q * wide + k] += from_left[block + k].astype(jnp.float32)

        @pl.when(a < last)
        def _():
            passed_on(from_right, left_send, left_recv, block, left_to).wait_recv()
            for k in range(wide):
                own[q * wide + k] += from_right[block + k].astype(jnp.float32)

        for k in range(wide):
            j = q * wide + k
            prior_arrival(j).wait_recv()
            total = own[j]
            total_out[j] = total.astype(jnp.bfloat16)
            gathered[block + k] = (
                prior_in[j].astype(jnp.float32) - (FROM_AVERAGE / n) * total).astype(jnp.bfloat16)

        @pl.when(a < last)
        def _():
            gather_copy(block, ag_right_send, right_to).start()

        @pl.when(a > 0)
        def _():
            gather_copy(block, ag_left_send, left_to).start()

        for k in range(wide):
            total_copy(q * wide + k).start()
    for j in range(n):
        write_out(a * per_chunk + j).start()

    def gather_step(t, carry):
        s, q = t // GATHER_PARTS + 1, t % GATHER_PARTS

        @pl.when(s <= a)
        def _():
            block = (a - s) * per_chunk + q * gather_wide
            gather_copy(block, ag_right_send, right_to).wait_recv()

            @pl.when(a < last)
            def _():
                gather_copy(block, ag_right_send, right_to).start()

            for k in range(gather_wide):
                write_out(block + k).start()

        @pl.when(s <= last - a)
        def _():
            block = (a + s) * per_chunk + q * gather_wide
            gather_copy(block, ag_left_send, left_to).wait_recv()

            @pl.when(a > 0)
            def _():
                gather_copy(block, ag_left_send, left_to).start()

            for k in range(gather_wide):
                write_out(block + k).start()

        return carry

    lax.fori_loop(0, last * GATHER_PARTS, gather_step, None)
    for j in range(n):
        total_arrival(j).wait_recv()
        pltpu.make_async_copy(total_in.at[j], totals_hbm.at[j], out_sem.at[j]).start()

    for j in range(n):
        pltpu.make_async_copy(total_in.at[j], totals_hbm.at[j], out_sem.at[j]).wait()
        prior_copy(j).wait_send()
        total_copy(j).wait_send()

    def drain(block, carry):
        write_out(block).wait()
        return carry

    lax.fori_loop(0, n * per_chunk, drain, None)

    def drain_sent(piece, carry):
        block = piece * wide
        rank = piece // PARTS
        above, below = rank > a, rank < a

        @pl.when(above)
        def _():
            passed_on(from_left, right_send, right_recv, block, right_to).wait_send()

        @pl.when(below)
        def _():
            passed_on(from_right, left_send, left_recv, block, left_to).wait_send()

        @pl.when(jnp.logical_not(above) & (a < last))
        def _():
            gather_copy(block, ag_right_send, right_to).wait_send()

        @pl.when(jnp.logical_not(below) & (a > 0))
        def _():
            gather_copy(block, ag_left_send, left_to).wait_send()

        return carry

    lax.fori_loop(0, n * PARTS, drain_sent, None)


def solution(mesh):
    n = mesh.shape["rep"]
    finer = Mesh(mesh.devices.reshape(n, n, -1), ("rep", "hi", "lo"))

    def per_device(base_weights, local_weights, outer_params, momentum):
        rows, width = base_weights.shape
        blocks = width // BLOCK
        per_chunk = blocks // n
        bf16, f32 = jnp.bfloat16, jnp.float32
        held = pltpu.VMEM((blocks, rows, BLOCK), bf16)
        eight = pltpu.VMEM((n, rows, BLOCK), bf16)
        owned = outer_params.shape
        dma = pltpu.SemaphoreType.DMA
        anywhere = pl.BlockSpec(memory_space=pl.ANY)
        pieces, gather_pieces = n * PARTS, n * GATHER_PARTS
        totals, new_weights = pl.pallas_call(
            functools.partial(kernel, n),
            out_shape=(
                jax.ShapeDtypeStruct((n, rows, BLOCK), bf16),
                jax.ShapeDtypeStruct((rows, width), bf16),
            ),
            in_specs=[anywhere] * 4,
            out_specs=(anywhere,) * 2,
            scratch_shapes=[
                pltpu.VMEM((rows, width), bf16), pltpu.VMEM((rows, width), bf16),
                pltpu.VMEM(owned, f32), pltpu.VMEM(owned, f32),
                pltpu.VMEM((per_chunk, rows, BLOCK), f32), held, held, held, held,
                eight, eight, eight, eight,
                dma((4,)), dma((n,)), dma((pieces,)), dma((pieces,)), dma((pieces,)), dma((pieces,)),
                dma((n,)), dma((n,)), dma((n,)), dma((n,)),
                dma((gather_pieces,)), dma((gather_pieces,)), dma((gather_pieces,)), dma((blocks,)),
            ],
            compiler_params=pltpu.CompilerParams(collective_id=0, has_side_effects=True),
        )(base_weights, local_weights[0], outer_params, momentum)
        average = totals.reshape(owned).astype(f32) / n
        new_momentum = MOMENTUM_DECAY * momentum + average
        new_outer = outer_params - OUTER_RATE * (average + MOMENTUM_DECAY * new_momentum)
        return new_outer, new_momentum, new_weights

    fsdp = ("hi", "lo")
    return jax.shard_map(
        per_device,
        mesh=finer,
        in_specs=(P(fsdp, None), P("rep", fsdp, None), P("rep", fsdp), P("rep", fsdp)),
        out_specs=(P("rep", fsdp), P("rep", fsdp), P(fsdp, None)),
        check_vma=False,
    )
```

time: 90.9 us -> 85.5 us (0.941)
  the two profiles are of different devices: /device:TPU:16 before, /device:TPU:8 now
where the time goes in v2:
time: 85.5 us; the launch traced here: 85.3 us
  Pallas kernels  81.8 us (96%)
  other arithmetic  1.88 us (2%)
  local copies, waits for them, and re-layouts  0.98 us (1%)
    pallas_call x1, Pallas kernels, per_device(): pl.pallas_call(functools.partial(kernel, n), out_shape=(jax.ShapeDtypeStr...  81.8 us

profile of v2, /device:TPU:8, one launch (start us, length us, event | category | flops | bytes accessed | tf_op | source)
XLA Modules:
  0.0 85.3 jit_solution(1071348404179332143)
XLA Ops:
  0.6 0.0 copy-start.1
  0.6 81.8 %shard_map.67 = (bf16[8,64,128]{2,1,0:T(8,128)(2,1)}, bf16[64,8192]{1,0:T(8,128)(2,1)}) custom-call(bf16[64,8192]{1,0:T(8,128)(2,1)} %base_hbm.1, bf16[64,8192]{1,0:T(8,128)(2,1)} %bitcast.9, f32[512,128]{1,0:T(8,128)} %outer_hbm.1, f32[512,128]{1,0:T(8,128)} %momentum_hbm.1), custom_call_target="tpu_custom_call" | custom-call | tf_op jit(solution)/shard_map/pallas_call | solution.py:303
  82.4 0.0 copy-start
  82.4 0.0 copy-start.2
  82.4 1.0 %convert_multiply_fusion = f32[8,64,128]{2,1,0:T(8,128)S(1)} fusion(bf16[8,64,128]{2,1,0:T(8,128)(2,1)} %get-tuple-element.5), kind=kLoop, calls=%fused_computation.4 | loop fusion | flops 131072 | bytes 393216 | tf_op jit(solution)/shard_map/div | solution.py:322
  83.5 0.0 copy-done.1
  83.5 0.0 copy-done
  83.5 0.9 %fusion.1 = (f32[512,128]{1,0:T(8,128)}, f32[512,128]{1,0:T(8,128)}) fusion(f32[512,128]{1,0:T(8,128)S(1)} %copy-done, f32[8,64,128]{2,1,0:T(8,128)S(1)} %convert_multiply_fusion, f32[512,128]{1,0:T(8,128)S(1)} %copy-done.1), kind=kLoop, calls=%fused_computation.3 | loop fusion | flops 393216 | bytes 1310720 | tf_op jit(solution)/shard_map/sub | solution.py:324
  84.3 0.0 copy-done.2
  84.3 1.0 %copy.8 = bf16[64,8192]{1,0:T(8,128)(2,1)} copy(bf16[64,8192]{1,0:T(8,128)(2,1)S(1)} %copy-done.2) | data formatting | bytes 2097152
Async XLA Ops:
  0.6 82.8 %copy-start.1 = (f32[512,128]{1,0:T(8,128)S(1)}, f32[512,128]{1,0:T(8,128)}, u32[]{:S(2)}) copy-start(f32[512,128]{1,0:T(8,128)} %momentum_hbm.1) | copy-start | bytes 786436
  82.4 1.1 %copy-start = (f32[512,128]{1,0:T(8,128)S(1)}, f32[512,128]{1,0:T(8,128)}, u32[]{:S(2)}) copy-start(f32[512,128]{1,0:T(8,128)} %outer_hbm.1) | copy-start | bytes 786436
  82.4 1.9 %copy-start.2 = (bf16[64,8192]{1,0:T(8,128)(2,1)S(1)}, bf16[64,8192]{1,0:T(8,128)(2,1)}, u32[]{:S(2)}) copy-start(bf16[64,8192]{1,0:T(8,128)(2,1)} %get-tuple-element.14) | copy-start | bytes 3145732

commit v3 on v2

--- a/solution.py
+++ b/solution.py
@@ -19,15 +19,16 @@
 FROM_AVERAGE = OUTER_RATE * (1.0 + MOMENTUM_DECAY)
 
 PARTS = 4
-LAG = 4
+LAG = 5
 GATHER_PARTS = 4
-
-
-def kernel(n, base_hbm, local_hbm, outer_hbm, momentum_hbm, totals_hbm, weights_hbm,
-           base, local, outer, momentum,
+ROUND_STEPS = (4, 6, 8, 11, 15, 17)
+
+
+def kernel(n, base_hbm, local_hbm, outer_hbm, momentum_hbm, averages_hbm, weights_hbm,
+           base, local, outer, momentum, average,
            own, sums, from_left, from_right, gathered, prior_out, prior_in, total_out, total_in,
            in_sem, out_sem, right_send, right_recv, left_send, left_recv,
-           prior_send, prior_recv, total_send, total_recv, ag_right_send, ag_left_send, ag_recv, weights_sem):
+           prior_send, prior_recv, total_send, total_recv, ag_right_send, ag_left_send, ag_recv, weights_sem, known):
     a, b, l = lax.axis_index("rep"), lax.axis_index("hi"), lax.axis_index("lo")
     last = n - 1
     per_chunk = own.shape[0]
@@ -56,21 +57,24 @@
     for copy in ins:
         copy.start()
 
+    ring_z, ring_x, ring_y = 2 * n, n // 2, n // 2
+    z, x, y, core = b // ring_x * n + a, b % ring_x, l // 2, l % 2
+
+    def at(dz=0, dx=0, dy=0, other=False):
+        to_z = (z + dz + ring_z) % ring_z
+        return (to_z % n, to_z // n * ring_x + (x + dx) % ring_x,
+                (y + dy) % ring_y * 2 + (1 - core if other else core))
+
+    def signal(sem, places):
+        for place in places:
+            pl.semaphore_signal(sem, inc=1, device_id=place, device_id_type=MESH)
+
+    along_x = [at(dx=d) for d in range(1, ring_x)]
+    along_y = [at(dy=d) for d in range(1, ring_y)]
+    rounds = [along_x, [at(other=True)]] + [[at(dz=d), at(dz=-d)] for d in (1, 2, 4, 1)]
+    greeted = [at(dz=1), at(dz=-1), at(other=True)] + along_x + along_y
     barrier = pltpu.get_barrier_semaphore()
-
-    @pl.when(a > 0)
-    def _():
-        pl.semaphore_signal(barrier, inc=1, device_id={"rep": a - 1}, device_id_type=MESH)
-
-    @pl.when(a < last)
-    def _():
-        pl.semaphore_signal(barrier, inc=1, device_id={"rep": a + 1}, device_id_type=MESH)
-
-    for j in range(n):
-        pl.semaphore_signal(barrier, inc=1, device_id=(root, a, j), device_id_type=MESH)
-        pl.semaphore_signal(barrier, inc=1, device_id=(b, mine, j), device_id_type=MESH)
-
-    greeted = 2 * n + 2 - (a == 0).astype(jnp.int32) - (a == last).astype(jnp.int32)
+    signal(barrier, greeted)
 
     def prior_copy(j):
         return pltpu.make_async_remote_copy(
@@ -109,9 +113,8 @@
     for j in range(n):
         part = pl.ds(j * rows, rows)
         prior_out[j] = (outer[part, :] - FROM_MOMENTUM * momentum[part, :]).astype(jnp.bfloat16)
-    pl.semaphore_wait(barrier, greeted)
-    for j in range(n):
-        prior_copy(j).start()
+    pl.semaphore_wait(barrier, len(greeted))
+    signal(known.at[0], rounds[0])
     ins[2].wait()
     ins[3].wait()
 
@@ -152,6 +155,15 @@
 
     def step(t, carry):
         u, v = t - a * LAG, t - (last - a) * LAG
+        for k in range(len(rounds)):
+            @pl.when(t == ROUND_STEPS[k])
+            def _():
+                pl.semaphore_wait(known.at[k], len(rounds[k]))
+                if k + 1 < len(rounds):
+                    signal(known.at[k + 1], rounds[k + 1])
+                else:
+                    for j in range(n):
+                        prior_copy(j).start()
 
         @pl.when((u >= 0) & (u < right_count))
         def _():
@@ -214,8 +226,43 @@
     for j in range(n):
         write_out(a * per_chunk + j).start()
 
+    def passed_sent(rank, q):
+        block = rank * per_chunk + q * wide
+
+        @pl.when(rank > a)
+        def _():
+            passed_on(from_left, right_send, right_recv, block, right_to).wait_send()
+
+        @pl.when(rank < a)
+        def _():
+            passed_on(from_right, left_send, left_recv, block, left_to).wait_send()
+
+    def gather_sent(s, q):
+        @pl.when((s <= a) & (a < last))
+        def _():
+            gather_copy((a - s) * per_chunk + q * gather_wide, ag_right_send, right_to).wait_send()
+
+        @pl.when((s <= last - a) & (a > 0))
+        def _():
+            gather_copy((a + s) * per_chunk + q * gather_wide, ag_left_send, left_to).wait_send()
+
+    def gather_written(s, q):
+        @pl.when(s <= a)
+        def _():
+            for k in range(gather_wide):
+                write_out((a - s) * per_chunk + q * gather_wide + k).wait()
+
+        @pl.when((s <= last - a) & (s > 0))
+        def _():
+            for k in range(gather_wide):
+                write_out((a + s) * per_chunk + q * gather_wide + k).wait()
+
     def gather_step(t, carry):
         s, q = t // GATHER_PARTS + 1, t % GATHER_PARTS
+        passed_sent(s - 1, q)
+        pl.when(s == last)(lambda: passed_sent(s, q))
+        pl.when(s >= 3)(lambda: gather_sent(s - 2, q))
+        gather_written(s - 1, q)
 
         @pl.when(s <= a)
         def _():
@@ -246,43 +293,19 @@
     lax.fori_loop(0, last * GATHER_PARTS, gather_step, None)
     for j in range(n):
         total_arrival(j).wait_recv()
-        pltpu.make_async_copy(total_in.at[j], totals_hbm.at[j], out_sem.at[j]).start()
-
-    for j in range(n):
-        pltpu.make_async_copy(total_in.at[j], totals_hbm.at[j], out_sem.at[j]).wait()
+        average[pl.ds(j * rows, rows), :] = total_in[j].astype(jnp.float32) / n
+    leaving = pltpu.make_async_copy(average, averages_hbm, out_sem.at[0])
+    leaving.start()
+
+    for j in range(n):
         prior_copy(j).wait_send()
         total_copy(j).wait_send()
-
-    def drain(block, carry):
-        write_out(block).wait()
-        return carry
-
-    lax.fori_loop(0, n * per_chunk, drain, None)
-
-    def drain_sent(piece, carry):
-        block = piece * wide
-        rank = piece // PARTS
-        above, below = rank > a, rank < a
-
-        @pl.when(above)
-        def _():
-            passed_on(from_left, right_send, right_recv, block, right_to).wait_send()
-
-        @pl.when(below)
-        def _():
-            passed_on(from_right, left_send, left_recv, block, left_to).wait_send()
-
-        @pl.when(jnp.logical_not(above) & (a < last))
-        def _():
-            gather_copy(block, ag_right_send, right_to).wait_send()
-
-        @pl.when(jnp.logical_not(below) & (a > 0))
-        def _():
-            gather_copy(block, ag_left_send, left_to).wait_send()
-
-        return carry
-
-    lax.fori_loop(0, n * PARTS, drain_sent, None)
+    for q in range(GATHER_PARTS):
+        gather_sent(0, q)
+        gather_sent(last - 1, q)
+        gather_sent(last, q)
+        gather_written(last, q)
+    leaving.wait()
 
 
 def solution(mesh):
@@ -300,26 +323,26 @@
         dma = pltpu.SemaphoreType.DMA
         anywhere = pl.BlockSpec(memory_space=pl.ANY)
         pieces, gather_pieces = n * PARTS, n * GATHER_PARTS
-        totals, new_weights = pl.pallas_call(
+        average, new_weights = pl.pallas_call(
             functools.partial(kernel, n),
             out_shape=(
-                jax.ShapeDtypeStruct((n, rows, BLOCK), bf16),
+                jax.ShapeDtypeStruct(owned, f32),
                 jax.ShapeDtypeStruct((rows, width), bf16),
             ),
             in_specs=[anywhere] * 4,
             out_specs=(anywhere,) * 2,
             scratch_shapes=[
                 pltpu.VMEM((rows, width), bf16), pltpu.VMEM((rows, width), bf16),
-                pltpu.VMEM(owned, f32), pltpu.VMEM(owned, f32),
+                pltpu.VMEM(owned, f32), pltpu.VMEM(owned, f32), pltpu.VMEM(owned, f32),
                 pltpu.VMEM((per_chunk, rows, BLOCK), f32), held, held, held, held,
                 eight, eight, eight, eight,
                 dma((4,)), dma((n,)), dma((pieces,)), dma((pieces,)), dma((pieces,)), dma((pieces,)),
                 dma((n,)), dma((n,)), dma((n,)), dma((n,)),
                 dma((gather_pieces,)), dma((gather_pieces,)), dma((gather_pieces,)), dma((blocks,)),
+                pltpu.SemaphoreType.REGULAR((6,)),
             ],
             compiler_params=pltpu.CompilerParams(collective_id=0, has_side_effects=True),
         )(base_weights, local_weights[0], outer_params, momentum)
-        average = totals.reshape(owned).astype(f32) / n
         new_momentum = MOMENTUM_DECAY * momentum + average
         new_outer = outer_params - OUTER_RATE * (average + MOMENTUM_DECAY * new_momentum)
         return new_outer, new_momentum, new_weights

time: 85.5 us -> 83.2 us (0.973)
  the two profiles are of different devices: /device:TPU:8 before, /device:TPU:4 now
where the time goes in v3:
time: 83.2 us; the launch traced here: 83.1 us
  Pallas kernels  79.5 us (96%)
  other arithmetic  1.89 us (2%)
  local copies, waits for them, and re-layouts  0.98 us (1%)
    pallas_call x1, Pallas kernels, per_device(): pl.pallas_call(functools.partial(kernel, n), out_shape=(jax.ShapeDtypeStr...  79.5 us
    sub x1, other arithmetic, per_device(): outer_params - OUTER_RATE * (average + MOMENTUM_DECAY * new_momentum)  1.89 us

profile of v3, /device:TPU:4, one launch (start us, length us, event | category | flops | bytes accessed | tf_op | source)
XLA Modules:
  0.0 83.1 jit_solution(9381767638502814152)
XLA Ops:
  0.6 0.0 copy-start
  0.6 0.0 copy-start.1
  0.7 79.5 %shard_map.67 = (f32[512,128]{1,0:T(8,128)}, bf16[64,8192]{1,0:T(8,128)(2,1)}) custom-call(bf16[64,8192]{1,0:T(8,128)(2,1)} %base_hbm.1, bf16[64,8192]{1,0:T(8,128)(2,1)} %bitcast.1, f32[512,128]{1,0:T(8,128)} %outer_hbm.1, f32[512,128]{1,0:T(8,128)} %momentum_hbm.1), custom_call_target="tpu_custom_call" | custom-call | tf_op jit(solution)/shard_map/pallas_call | solution.py:326
  80.2 0.0 copy-start.2
  80.2 0.0 copy-done
  80.2 0.0 copy-done.1
  80.2 1.9 %multiply_subtract_fusion = (f32[512,128]{1,0:T(8,128)}, f32[512,128]{1,0:T(8,128)}) fusion(f32[512,128]{1,0:T(8,128)S(1)} %copy-done, f32[512,128]{1,0:T(8,128)} %get-tuple-element.5, f32[512,128]{1,0:T(8,128)S(1)} %copy-done.1), kind=kLoop, calls=%fused_computation | loop fusion | flops 393216 | bytes 1310720 | tf_op jit(solution)/shard_map/sub | solution.py:347
  82.1 0.0 copy-done.2
  82.1 1.0 %copy.8 = bf16[64,8192]{1,0:T(8,128)(2,1)} copy(bf16[64,8192]{1,0:T(8,128)(2,1)S(1)} %copy-done.2) | data formatting | bytes 2097152
Async XLA Ops:
  0.6 79.6 %copy-start = (f32[512,128]{1,0:T(8,128)S(1)}, f32[512,128]{1,0:T(8,128)}, u32[]{:S(2)}) copy-start(f32[512,128]{1,0:T(8,128)} %outer_hbm.1) | copy-start | bytes 786436
  0.6 79.6 %copy-start.1 = (f32[512,128]{1,0:T(8,128)S(1)}, f32[512,128]{1,0:T(8,128)}, u32[]{:S(2)}) copy-start(f32[512,128]{1,0:T(8,128)} %momentum_hbm.1) | copy-start | bytes 786436
  80.2 1.9 %copy-start.2 = (bf16[64,8192]{1,0:T(8,128)(2,1)S(1)}, bf16[64,8192]{1,0:T(8,128)(2,1)}, u32[]{:S(2)}) copy-start(bf16[64,8192]{1,0:T(8,128)(2,1)} %get-tuple-element.14) | copy-start | bytes 3145732

commit v4 on v3

--- a/solution.py
+++ b/solution.py
@@ -21,7 +21,7 @@
 PARTS = 4
 LAG = 5
 GATHER_PARTS = 4
-ROUND_STEPS = (4, 6, 8, 11, 15, 17)
+ROUND_STEPS = (4, 6, 8, 13, 15)
 
 
 def kernel(n, base_hbm, local_hbm, outer_hbm, momentum_hbm, averages_hbm, weights_hbm,
@@ -71,8 +71,8 @@
 
     along_x = [at(dx=d) for d in range(1, ring_x)]
     along_y = [at(dy=d) for d in range(1, ring_y)]
-    rounds = [along_x, [at(other=True)]] + [[at(dz=d), at(dz=-d)] for d in (1, 2, 4, 1)]
-    greeted = [at(dz=1), at(dz=-1), at(other=True)] + along_x + along_y
+    rounds = [along_x, [at(other=True)]] + [[at(dz=d) for d in turn] for turn in ((1, -1, 2, -2), (4, -4), (2, -2))]
+    greeted = [at(dz=d) for d in (1, -1, 2, -2)] + [at(other=True)] + along_x + along_y
     barrier = pltpu.get_barrier_semaphore()
     signal(barrier, greeted)
 
@@ -339,7 +339,7 @@
                 dma((4,)), dma((n,)), dma((pieces,)), dma((pieces,)), dma((pieces,)), dma((pieces,)),
                 dma((n,)), dma((n,)), dma((n,)), dma((n,)),
                 dma((gather_pieces,)), dma((gather_pieces,)), dma((gather_pieces,)), dma((blocks,)),
-                pltpu.SemaphoreType.REGULAR((6,)),
+                pltpu.SemaphoreType.REGULAR((5,)),
             ],
             compiler_params=pltpu.CompilerParams(collective_id=0, has_side_effects=True),
         )(base_weights, local_weights[0], outer_params, momentum)

time: 83.2 us -> 82.1 us (0.987)
  the two profiles are of different devices: /device:TPU:4 before, /device:TPU:8 now
where the time goes in v4:
time: 82.1 us; the launch traced here: 81.9 us
  Pallas kernels  78.4 us (95%)
  other arithmetic  1.89 us (2%)
  local copies, waits for them, and re-layouts  0.98 us (1%)
    pallas_call x1, Pallas kernels, per_device(): pl.pallas_call(functools.partial(kernel, n), out_shape=(jax.ShapeDtypeStr...  78.4 us
    sub x1, other arithmetic, per_device(): outer_params - OUTER_RATE * (average + MOMENTUM_DECAY * new_momentum)  1.89 us

profile of v4, /device:TPU:8, one launch (start us, length us, event | category | flops | bytes accessed | tf_op | source)
XLA Modules:
  0.0 81.9 jit_solution(12180671079016013513)
XLA Ops:
  0.6 0.0 copy-start
  0.6 0.0 copy-start.1
  0.7 78.4 %shard_map.67 = (f32[512,128]{1,0:T(8,128)}, bf16[64,8192]{1,0:T(8,128)(2,1)}) custom-call(bf16[64,8192]{1,0:T(8,128)(2,1)} %base_hbm.1, bf16[64,8192]{1,0:T(8,128)(2,1)} %bitcast.1, f32[512,128]{1,0:T(8,128)} %outer_hbm.1, f32[512,128]{1,0:T(8,128)} %momentum_hbm.1), custom_call_target="tpu_custom_call" | custom-call | tf_op jit(solution)/shard_map/pallas_call | solution.py:326
  79.0 0.0 copy-start.2
  79.0 0.0 copy-done
  79.0 0.0 copy-done.1
  79.1 1.9 %multiply_subtract_fusion = (f32[512,128]{1,0:T(8,128)}, f32[512,128]{1,0:T(8,128)}) fusion(f32[512,128]{1,0:T(8,128)S(1)} %copy-done, f32[512,128]{1,0:T(8,128)} %get-tuple-element.5, f32[512,128]{1,0:T(8,128)S(1)} %copy-done.1), kind=kLoop, calls=%fused_computation | loop fusion | flops 393216 | bytes 1310720 | tf_op jit(solution)/shard_map/sub | solution.py:347
  80.9 0.0 copy-done.2
  80.9 1.0 %copy.8 = bf16[64,8192]{1,0:T(8,128)(2,1)} copy(bf16[64,8192]{1,0:T(8,128)(2,1)S(1)} %copy-done.2) | data formatting | bytes 2097152
Async XLA Ops:
  0.6 78.4 %copy-start = (f32[512,128]{1,0:T(8,128)S(1)}, f32[512,128]{1,0:T(8,128)}, u32[]{:S(2)}) copy-start(f32[512,128]{1,0:T(8,128)} %outer_hbm.1) | copy-start | bytes 786436
  0.6 78.4 %copy-start.1 = (f32[512,128]{1,0:T(8,128)S(1)}, f32[512,128]{1,0:T(8,128)}, u32[]{:S(2)}) copy-start(f32[512,128]{1,0:T(8,128)} %momentum_hbm.1) | copy-start | bytes 786436
  79.0 1.9 %copy-start.2 = (bf16[64,8192]{1,0:T(8,128)(2,1)S(1)}, bf16[64,8192]{1,0:T(8,128)(2,1)}, u32[]{:S(2)}) copy-start(bf16[64,8192]{1,0:T(8,128)(2,1)} %get-tuple-element.14) | copy-start | bytes 3145732
